TPU v7x, 32 devices: a whole 2x2x4 slice. The times are simulated.
32 devices in a mesh: fsdp: 8 (over y, x, core), replica: 4 (over z).
Axes of the slice: x: 2, y: 2, z: 4, core: 2. Of those that a mesh axis runs over, the one named last changes fastest.
Arguments:
- inputs: bfloat16 [8, 512, 768], P('fsdp', 'replica'), may hold values from -6 to 6
- cotangent: bfloat16 [8, 512, 768], P('fsdp', 'replica'), may hold values from -6 to 6
- segments: int32 [8, 512], P('fsdp'), may hold values from 0 to 2, never falling along the last dimension, each value on 1 to 256 neighbouring positions
- w_qkv_state: float32 [3, 768, 2304], P(None, 'fsdp'), as said below
- b_qkv_state: float32 [3, 2, 768], P(None, None, 'fsdp')
- w_o_state: float32 [3, 768, 768], P(None, 'fsdp')
- w_fc_state: float32 [3, 768, 3072], P(None, 'fsdp')
- b_fc_state: float32 [3, 3072], P(None, 'fsdp')
- w_pr_state: float32 [3, 3072, 768], P(None, 'fsdp')
- vec_state: float32 [3, 6, 768], P(None, None, 'fsdp'), as said below
Outputs:
- outputs: bfloat16 [8, 512, 768], P('fsdp', 'replica')
- input_grad: bfloat16 [8, 512, 768], P('fsdp', 'replica')
- grad_w_qkv: float32 [768, 2304], P('fsdp')
- grad_b_qkv: float32 [2, 768], P(None, 'fsdp')
- grad_w_o: float32 [768, 768], P('fsdp')
- grad_w_fc: float32 [768, 3072], P('fsdp')
- grad_b_fc: float32 [3072], P('fsdp')
- grad_w_pr: float32 [3072, 768], P('fsdp')
- grad_vectors: float32 [6, 768], P(None, 'fsdp')
- new_w_qkv: float32 [3, 768, 2304], P(None, 'fsdp')
- new_b_qkv: float32 [3, 2, 768], P(None, None, 'fsdp')
- new_w_o: float32 [3, 768, 768], P(None, 'fsdp')
- new_w_fc: float32 [3, 768, 3072], P(None, 'fsdp')
- new_b_fc: float32 [3, 3072], P(None, 'fsdp')
- new_w_pr: float32 [3, 3072, 768], P(None, 'fsdp')
- new_vectors: float32 [3, 6, 768], P(None, None, 'fsdp')
Inputs may be any that keep to these rules, and one draw needn't show every extreme that they name: `w_qkv_state`: slice 0 of each state is the parameter, slice 1 its first moment, slice 2 its second moment, which is positive. `vec_state`: as for w_qkv_state.
All inputs are finite; a program needn't handle non-finite values.
Results may differ from a plain program's by a relative error of at most 0.012.
Values may be sent and summed in bfloat16 or wider, within the bound.
A program may use at most 192 MiB of HBM per device.

v0:
```python
import math

import jax
import jax.numpy as jnp
from jax import lax
from jax.sharding import PartitionSpec as P

HD = 64
STEP = 2


NORM_EPSILON = 1e-05
ADAM_EPSILON = 1e-08
BETA_FIRST = 0.9
BETA_SECOND = 0.95
LEARN_RATE = 0.06
WEIGHT_DECAY = 0.1
GELU_SCALE = math.sqrt(2.0 / math.pi)
SCORE_SCALE = 0.125


def layer_norm(values, norm_gain, norm_bias):
    center = values - jnp.mean(values, -1, keepdims=True)
    scaler = lax.rsqrt(jnp.mean(center * center, -1, keepdims=True) + NORM_EPSILON)
    normed = center * scaler
    return (normed * norm_gain + norm_bias, normed, scaler)


def norm_back(grad_out, norm_gain, normed, scaler):
    scaled = grad_out * norm_gain
    return scaler * (
        scaled
        - jnp.mean(scaled, -1, keepdims=True)
        - normed * jnp.mean(scaled * normed, -1, keepdims=True)
    )


def gelu_parts(pre_act):
    inner = GELU_SCALE * (pre_act + 0.044715 * pre_act * pre_act * pre_act)
    tangent = jnp.tanh(inner)
    activ = 0.5 * pre_act * (1.0 + tangent)
    slope = 0.5 * (1.0 + tangent) + 0.5 * pre_act * (1.0 - tangent * tangent) * GELU_SCALE * (
        1.0 + 3.0 * 0.044715 * pre_act * pre_act
    )
    return (activ, slope)


def adamw(state, grad, decay):
    first = BETA_FIRST * state[1] + (1.0 - BETA_FIRST) * grad
    second = BETA_SECOND * state[2] + (1.0 - BETA_SECOND) * grad * grad
    first_hat = first / (1.0 - BETA_FIRST**STEP)
    second_hat = second / (1.0 - BETA_SECOND**STEP)
    weight = state[0] - LEARN_RATE * (
        first_hat / (jnp.sqrt(second_hat) + ADAM_EPSILON) + decay * state[0]
    )
    return jnp.stack([weight, first, second])


def split_heads(query, key_value):
    width = query.shape[1]
    heads = width // HD
    query_h = query.reshape(query.shape[0], heads, HD)
    key_h = key_value[:, :width].reshape(key_value.shape[0], heads, HD)
    value_h = key_value[:, width:].reshape(key_value.shape[0], heads, HD)
    return (query_h, key_h, value_h)


def masked_scores(query_h, key_h, seg_query, seg_key, pos_query, pos_key):
    allowed = (seg_query[:, None] == seg_key[None, :]) & (pos_key[None, :] <= pos_query[:, None])
    scores = (
        jnp.einsum("qhd,khd->hqk", query_h, key_h, preferred_element_type=jnp.float32) * SCORE_SCALE
    )
    return jnp.where(allowed[None], scores, -1e30)


def attend_forward(query, key_value, seg_query, seg_key, pos_query, pos_key):
    query_h, key_h, value_h = split_heads(query, key_value)
    scores = masked_scores(query_h, key_h, seg_query, seg_key, pos_query, pos_key)
    top = jnp.max(scores, -1, keepdims=True)
    log_norm = top + jnp.log(jnp.sum(jnp.exp(scores - top), -1, keepdims=True))
    prob = jnp.exp(scores - log_norm).astype(jnp.bfloat16)
    attended = jnp.einsum("hqk,khd->qhd", prob, value_h, preferred_element_type=jnp.float32)
    return (attended.reshape(query.shape[0], query.shape[1]).astype(jnp.bfloat16), log_norm)


def attend_backward(
    query, key_value, seg_query, seg_key, pos_query, pos_key, log_norm, attended, grad_att
):
    query_h, key_h, value_h = split_heads(query, key_value)
    rows = query.shape[0]
    heads = query_h.shape[1]
    scores = masked_scores(query_h, key_h, seg_query, seg_key, pos_query, pos_key)
    prob_f = jnp.exp(scores - log_norm)
    prob = prob_f.astype(jnp.bfloat16)
    grad_att_h = grad_att.reshape(rows, heads, HD)
    delta = jnp.sum(
        grad_att_h.astype(jnp.float32) * attended.reshape(rows, heads, HD).astype(jnp.float32), -1
    )
    grad_prob = jnp.einsum("qhd,khd->hqk", grad_att_h, value_h, preferred_element_type=jnp.float32)
    grad_score = (prob_f * (grad_prob - delta.T[..., None]) * SCORE_SCALE).astype(jnp.bfloat16)
    grad_query = jnp.einsum("hqk,khd->qhd", grad_score, key_h, preferred_element_type=jnp.float32)
    grad_key = jnp.einsum("hqk,qhd->khd", grad_score, query_h, preferred_element_type=jnp.float32)
    grad_value = jnp.einsum("hqk,qhd->khd", prob, grad_att_h, preferred_element_type=jnp.float32)
    key_rows = key_value.shape[0]
    grad_kv = jnp.concatenate([grad_key.reshape(key_rows, -1), grad_value.reshape(key_rows, -1)], 1)
    return (grad_query.reshape(rows, -1), grad_kv)


def body(
    inputs,
    cotangent,
    segments,
    w_qkv_state,
    b_qkv_state,
    w_o_state,
    w_fc_state,
    b_fc_state,
    w_pr_state,
    vec_state,
):
    gathered = (
        lax.all_gather(w_qkv_state[0].astype(jnp.bfloat16), "fsdp", axis=0, tiled=True),
        lax.all_gather(b_qkv_state[0].astype(jnp.bfloat16), "fsdp", axis=1, tiled=True),
        lax.all_gather(w_o_state[0].astype(jnp.bfloat16), "fsdp", axis=0, tiled=True),
        lax.all_gather(w_fc_state[0].astype(jnp.bfloat16), "fsdp", axis=0, tiled=True),
        lax.all_gather(b_fc_state[0].astype(jnp.bfloat16), "fsdp", axis=0, tiled=True),
        lax.all_gather(w_pr_state[0].astype(jnp.bfloat16), "fsdp", axis=0, tiled=True),
        lax.all_gather(vec_state[0].astype(jnp.bfloat16), "fsdp", axis=1, tiled=True),
    )
    w_qkv, b_qkv, w_out, w_fc, b_fc, w_pr, vectors = gathered
    vector_f = vectors.astype(jnp.float32)
    bias_row = jnp.concatenate([b_qkv[0], jnp.zeros_like(b_qkv[0]), b_qkv[1]]).astype(jnp.float32)
    seq_count, span, width = inputs.shape
    full_len = segments.shape[1]
    row_count = seq_count * span
    pos_all = jnp.arange(full_len, dtype=jnp.int32)
    hidden = inputs.reshape(row_count, width).astype(jnp.float32)
    attn_in_f, normed_one, scale_one = layer_norm(hidden, vector_f[0], vector_f[1])
    attn_in = attn_in_f.astype(jnp.bfloat16)
    projected = (jnp.dot(attn_in, w_qkv, preferred_element_type=jnp.float32) + bias_row).astype(
        jnp.bfloat16
    )
    queries = projected[:, :width].reshape(seq_count, span, width)
    key_value = projected[:, width:].reshape(seq_count, span, 2 * width)
    key_value_all = lax.all_gather(key_value, "replica", axis=1, tiled=True)
    offset = lax.axis_index("replica") * span
    pos_query = offset + jnp.arange(span, dtype=jnp.int32)
    seg_query = lax.dynamic_slice_in_dim(segments, offset, span, 1)

    def forward_one(element):
        return attend_forward(element[0], element[1], element[2], element[3], pos_query, pos_all)

    attended, log_norm = lax.map(forward_one, (queries, key_value_all, seg_query, segments))
    attended_rows = attended.reshape(row_count, width)
    mixed = hidden + jnp.dot(attended_rows, w_out, preferred_element_type=jnp.float32) + vector_f[2]
    ffn_in_f, normed_two, scale_two = layer_norm(mixed, vector_f[3], vector_f[4])
    ffn_in = ffn_in_f.astype(jnp.bfloat16)
    pre_act = jnp.dot(ffn_in, w_fc, preferred_element_type=jnp.float32) + b_fc.astype(jnp.float32)
    activ, slope = gelu_parts(pre_act)
    activ_b = activ.astype(jnp.bfloat16)
    result = mixed + jnp.dot(activ_b, w_pr, preferred_element_type=jnp.float32) + vector_f[5]
    back_weights = (
        lax.all_gather(w_qkv_state[0].astype(jnp.bfloat16), "fsdp", axis=0, tiled=True),
        lax.all_gather(b_qkv_state[0].astype(jnp.bfloat16), "fsdp", axis=1, tiled=True),
        lax.all_gather(w_o_state[0].astype(jnp.bfloat16), "fsdp", axis=0, tiled=True),
        lax.all_gather(w_fc_state[0].astype(jnp.bfloat16), "fsdp", axis=0, tiled=True),
        lax.all_gather(b_fc_state[0].astype(jnp.bfloat16), "fsdp", axis=0, tiled=True),
        lax.all_gather(w_pr_state[0].astype(jnp.bfloat16), "fsdp", axis=0, tiled=True),
        lax.all_gather(vec_state[0].astype(jnp.bfloat16), "fsdp", axis=1, tiled=True),
    )
    back_qkv, back_bias_qkv, back_out, back_fc, back_bias_fc, back_pr, back_vectors = back_weights
    back_vec_f = back_vectors.astype(jnp.float32)
    cot_rows = cotangent.reshape(row_count, width)
    cot_f = cot_rows.astype(jnp.float32)
    grad_w_pr = jnp.dot(activ_b.T, cot_rows, preferred_element_type=jnp.float32)
    grad_b_pr = jnp.sum(cot_f, 0)
    grad_pre = jnp.dot(cot_rows, back_pr.T, preferred_element_type=jnp.float32) * slope
    grad_pre_b = grad_pre.astype(jnp.bfloat16)
    grad_w_fc = jnp.dot(ffn_in.T, grad_pre_b, preferred_element_type=jnp.float32)
    grad_b_fc = jnp.sum(grad_pre, 0)
    grad_ffn = jnp.dot(grad_pre_b, back_fc.T, preferred_element_type=jnp.float32)
    grad_gain_two = jnp.sum(grad_ffn * normed_two, 0)
    grad_bias_two = jnp.sum(grad_ffn, 0)
    grad_mixed = cot_f + norm_back(grad_ffn, back_vec_f[3], normed_two, scale_two)
    grad_mixed_b = grad_mixed.astype(jnp.bfloat16)
    grad_w_out = jnp.dot(attended_rows.T, grad_mixed_b, preferred_element_type=jnp.float32)
    grad_b_out = jnp.sum(grad_mixed, 0)
    grad_att = jnp.dot(grad_mixed_b, back_out.T, preferred_element_type=jnp.float32).astype(
        jnp.bfloat16
    )
    grad_att = grad_att.reshape(seq_count, span, width)

    def backward_one(element):
        return attend_backward(
            element[0],
            element[1],
            element[2],
            element[3],
            pos_query,
            pos_all,
            element[4],
            element[5],
            element[6],
        )

    grad_query, grad_kv_part = lax.map(
        backward_one, (queries, key_value_all, seg_query, segments, log_norm, attended, grad_att)
    )
    grad_kv = lax.psum_scatter(grad_kv_part, "replica", scatter_dimension=1, tiled=True)
    grad_proj = jnp.concatenate([grad_query, grad_kv], 2).reshape(row_count, 3 * width)
    grad_proj_b = grad_proj.astype(jnp.bfloat16)
    grad_b_qkv = jnp.stack(
        [jnp.sum(grad_proj[:, :width], 0), jnp.sum(grad_proj[:, 2 * width :], 0)]
    )
    grad_w_qkv = jnp.dot(attn_in.T, grad_proj_b, preferred_element_type=jnp.float32)
    grad_in = jnp.dot(grad_proj_b, back_qkv.T, preferred_element_type=jnp.float32)
    grad_gain_one = jnp.sum(grad_in * normed_one, 0)
    grad_bias_one = jnp.sum(grad_in, 0)
    grad_input = grad_mixed + norm_back(grad_in, back_vec_f[0], normed_one, scale_one)
    grad_vec = jnp.stack(
        [grad_gain_one, grad_bias_one, grad_b_out, grad_gain_two, grad_bias_two, grad_b_pr]
    )
    shares = (
        lax.psum_scatter(grad_w_qkv, "fsdp", scatter_dimension=0, tiled=True),
        lax.psum_scatter(grad_b_qkv, "fsdp", scatter_dimension=1, tiled=True),
        lax.psum_scatter(grad_w_out, "fsdp", scatter_dimension=0, tiled=True),
        lax.psum_scatter(grad_w_fc, "fsdp", scatter_dimension=0, tiled=True),
        lax.psum_scatter(grad_b_fc, "fsdp", scatter_dimension=0, tiled=True),
        lax.psum_scatter(grad_w_pr, "fsdp", scatter_dimension=0, tiled=True),
        lax.psum_scatter(grad_vec, "fsdp", scatter_dimension=1, tiled=True),
    )
    matrix_parts = (
        lax.psum_scatter(shares[0], "replica", scatter_dimension=1, tiled=True),
        lax.psum_scatter(shares[2], "replica", scatter_dimension=1, tiled=True),
        lax.psum_scatter(shares[3], "replica", scatter_dimension=1, tiled=True),
        lax.psum_scatter(shares[5], "replica", scatter_dimension=1, tiled=True),
    )
    matrix_sums = (
        lax.all_gather(matrix_parts[0], "replica", axis=1, tiled=True),
        lax.all_gather(matrix_parts[1], "replica", axis=1, tiled=True),
        lax.all_gather(matrix_parts[2], "replica", axis=1, tiled=True),
        lax.all_gather(matrix_parts[3], "replica", axis=1, tiled=True),
    )
    small_sums = lax.psum((shares[1], shares[4], shares[6]), "replica")
    totals = (
        matrix_sums[0],
        small_sums[0],
        matrix_sums[1],
        matrix_sums[2],
        small_sums[1],
        matrix_sums[3],
        small_sums[2],
    )
    factor = float(row_count * lax.axis_size("fsdp") * lax.axis_size("replica")) ** (-0.5)
    grads = [total * factor for total in totals]
    new_w_qkv = adamw(w_qkv_state, grads[0], WEIGHT_DECAY)
    new_b_qkv = adamw(b_qkv_state, grads[1], 0.0)
    new_w_o = adamw(w_o_state, grads[2], WEIGHT_DECAY)
    new_w_fc = adamw(w_fc_state, grads[3], WEIGHT_DECAY)
    new_b_fc = adamw(b_fc_state, grads[4], 0.0)
    new_w_pr = adamw(w_pr_state, grads[5], WEIGHT_DECAY)
    new_vectors = adamw(vec_state, grads[6], 0.0)
    outputs = result.reshape(seq_count, span, width).astype(jnp.bfloat16)
    input_grad = grad_input.reshape(seq_count, span, width).astype(jnp.bfloat16)
    return (
        outputs,
        input_grad,
        grads[0],
        grads[1],
        grads[2],
        grads[3],
        grads[4],
        grads[5],
        grads[6],
        new_w_qkv,
        new_b_qkv,
        new_w_o,
        new_w_fc,
        new_b_fc,
        new_w_pr,
        new_vectors,
    )


def solution(mesh):
    in_specs = (
        P("fsdp", "replica", None),
        P("fsdp", "replica", None),
        P("fsdp", None),
        P(None, "fsdp", None),
        P(None, None, "fsdp"),
        P(None, "fsdp", None),
        P(None, "fsdp", None),
        P(None, "fsdp"),
        P(None, "fsdp", None),
        P(None, None, "fsdp"),
    )
    out_specs = (
        P("fsdp", "replica", None),
        P("fsdp", "replica", None),
        P("fsdp", None),
        P(None, "fsdp"),
        P("fsdp", None),
        P("fsdp", None),
        P("fsdp"),
        P("fsdp", None),
        P(None, "fsdp"),
        P(None, "fsdp", None),
        P(None, None, "fsdp"),
        P(None, "fsdp", None),
        P(None, "fsdp", None),
        P(None, "fsdp"),
        P(None, "fsdp", None),
        P(None, None, "fsdp"),
    )
    return jax.shard_map(body, mesh=mesh, in_specs=in_specs, out_specs=out_specs, check_vma=False)
```

profile of v0, /device:TPU:0, one launch (start us, length us, event | category | flops | bytes accessed | tf_op | source)
XLA Modules:
  0.0 831.8 jit_solution(4863553583682085700)
XLA Ops:
  7.2 2.0 bitcast_convert_fusion.2
  10.0 10.4 %all-gather.1 = bf16[8,96,6]{1,2,0:T(8,128)(2,1)S(1)} all-gather(bf16[1,96,6]{1,2,0:T(8,128)(2,1)S(1)} %fusion.85), channel_id=1, replica_groups=mesh['fsdp'=8,'replica'=4] {'fsdp'}, dimensions={0}, use_global_device_ids=true | all-gather | bytes 10368 | tf_op jit(solution)/shard_map/all_gather | solution.py:128
  21.2 8.9 %all-gather.2 = bf16[8,96,2]{1,2,0:T(2,128)(2,1)S(1)} all-gather(bf16[1,96,2]{1,2,0:T(2,128)(2,1)S(1)} %fusion.90), channel_id=1, replica_groups=mesh['fsdp'=8,'replica'=4] {'fsdp'}, dimensions={0}, use_global_device_ids=true | all-gather | bytes 3456 | tf_op jit(solution)/shard_map/all_gather | solution.py:123
  31.2 15.9 %all-gather.13.cloned.1.call-done = bf16[768,2304]{1,0:T(8,128)(2,1)} async-done(((bf16[96,2304]{1,0:T(8,128)(2,1)}), bf16[768,2304]{1,0:T(8,128)(2,1)}) %all-gather.13.cloned.1.call-update) | async-done | bytes 3538960 | tf_op jit(solution)/shard_map/all_gather | solution.py:122
  47.1 2.7 fusion
  52.3 2.2 bitcast_convert_fusion.1
  54.6 3.7 fusion.103
  60.8 8.9 %all-gather.3 = bf16[8,1,384]{2,1,0:T(2,128)(2,1)S(1)} all-gather(bf16[1,1,384]{2,1,0:T(2,128)(2,1)S(1)} %reshape.310), channel_id=1, replica_groups=mesh['fsdp'=8,'replica'=4] {'fsdp'}, dimensions={0}, use_global_device_ids=true | all-gather | bytes 6912 | tf_op jit(solution)/shard_map/all_gather | solution.py:126
  71.9 15.9 %all-gather.25.cloned.1.call-done = bf16[512,1536]{1,0:T(8,128)(2,1)} async-done(((bf16[128,1536]{1,0:T(8,128)(2,1)}), bf16[512,1536]{1,0:T(8,128)(2,1)}) %all-gather.25.cloned.1.call-update) | async-done | bytes 1572880 | tf_op jit(solution)/shard_map/all_gather | solution.py:145
  96.6 16.4 %all-gather.15.cloned.1.call-done = bf16[768,768]{1,0:T(8,128)(2,1)} async-done(((bf16[96,768]{1,0:T(8,128)(2,1)}), bf16[768,768]{1,0:T(8,128)(2,1)}) %all-gather.15.cloned.1.call-update) | async-done | bytes 1179664 | tf_op jit(solution)/shard_map/all_gather | solution.py:124
  116.1 38.1 %all-gather.17.cloned.1.call-done = bf16[768,3072]{1,0:T(8,128)(2,1)} async-done(((bf16[96,3072]{1,0:T(8,128)(2,1)}), bf16[768,3072]{1,0:T(8,128)(2,1)}) %all-gather.17.cloned.1.call-update) | async-done | bytes 4718608 | tf_op jit(solution)/shard_map/all_gather | solution.py:125
  154.2 3.3 convolution_add_fusion.1
  158.6 5.2 fusion.64
  164.1 32.1 %all-gather.19.cloned.1.call-done = bf16[3072,768]{0,1:T(8,128)(2,1)} async-done(((bf16[384,768]{0,1:T(8,128)(2,1)}), bf16[3072,768]{0,1:T(8,128)(2,1)}) %all-gather.19.cloned.1.call-update) | async-done | bytes 4718608 | tf_op jit(solution)/shard_map/all_gather | solution.py:127
  196.1 5.3 fusion.106
  201.5 5.0 multiply_reduce_fusion
  210.0 7.3 fusion.48
  217.4 2.7 convolution_convert_fusion
  222.9 2.4 multiply_convert_fusion
  229.6 46.7 %reduce-scatter.32.cloned.1.call-done = f32[384,768]{1,0:T(8,128)} async-done(((f32[3072,768]{1,0:T(8,128)}), f32[384,768]{1,0:T(8,128)}) %reduce-scatter.32.cloned.1.call-update) | async-done | bytes 1179664 | tf_op jit(solution)/shard_map/reduce_scatter | solution.py:229
  276.3 2.7 copy.107
  279.1 43.5 %reduce-scatter.26.cloned.1.call-done = f32[96,768]{1,0:T(8,128)} async-done(((f32[768,768]{1,0:T(8,128)}), f32[96,768]{1,0:T(8,128)}) %reduce-scatter.26.cloned.1.call-update) | async-done | bytes 294928 | tf_op jit(solution)/shard_map/reduce_scatter | solution.py:226
  324.6 78.4 %reduce-scatter.28.cloned.1.call-done = f32[96,3072]{1,0:T(8,128)} async-done(((f32[768,3072]{1,0:T(8,128)}), f32[96,3072]{1,0:T(8,128)}) %reduce-scatter.28.cloned.1.call-update) | async-done | bytes 1179664 | tf_op jit(solution)/shard_map/reduce_scatter | solution.py:227
  403.8 62.5 %reduce-scatter.22.cloned.1.call-done = f32[1,128,1536]{1,2,0:T(8,128)} async-done(((f32[1,512,1536]{1,2,0:T(8,128)}), f32[1,128,1536]{1,2,0:T(8,128)}) %reduce-scatter.22.cloned.1.call-update) | async-done | bytes 786448 | tf_op jit(solution)/shard_map/reduce_scatter | solution.py:209
  469.0 4.1 fusion.42
  474.2 4.2 fusion.22
  478.6 19.1 %reduce-scatter.40.cloned.1.call-done = f32[192,384]{1,0:T(8,128)} async-done(((f32[768,384]{1,0:T(8,128)}), f32[192,384]{1,0:T(8,128)}) %reduce-scatter.40.cloned.1.call-update) | async-done | bytes 294928
  498.2 2.8 copy.113
  502.3 24.3 %all-reduce = f32[3072]{0:T(1024)S(1)} all-reduce(f32[3072]{0:T(1024)S(1)} %copy-done.47), channel_id=11, replica_groups=mesh['fsdp'=8,'replica'=4] {'fsdp'}, use_global_device_ids=true, to_apply=%region_23.24.clone | all-reduce | flops 3072 | bytes 24576
  526.6 4.8 fusion.17
  531.4 18.4 %all_gather.50 = f32[96,768]{0,1:T(8,128)S(1)} all-gather(f32[96,192]{0,1:T(8,128)} %bitcast.372), channel_id=1, replica_groups=mesh['fsdp'=8,'replica'=4] {'replica'}, dimensions={1}, use_global_device_ids=true | all-gather | bytes 368640 | tf_op jit(solution)/shard_map/all_gather | solution.py:240
  551.5 4.6 reduce-scatter.30.cloned.1.call-done
  557.0 35.2 %reduce-scatter.36.cloned.1.call-done = f32[96,2]{1,0:T(8,128)} async-done(((f32[768,2]{1,0:T(8,128)}), f32[96,2]{1,0:T(8,128)}) %reduce-scatter.36.cloned.1.call-update) | async-done | bytes 784
  593.1 36.6 %reduce-scatter.42.cloned.1.call-done = f32[96,6]{1,0:T(8,128)} async-done(((f32[768,6]{1,0:T(8,128)}), f32[96,6]{1,0:T(8,128)}) %reduce-scatter.42.cloned.1.call-update) | async-done | bytes 2320
  630.5 11.8 %all-reduce.1 = (f32[2,96]{1,0:T(2,128)S(1)}, f32[384]{0:T(512)S(1)}, f32[6,96]{1,0:T(8,128)S(1)}) all-reduce(f32[2,96]{1,0:T(2,128)S(1)} %copy.104, f32[384]{0:T(512)S(1)} %dynamic-slice.5, f32[6,96]{1,0:T(8,128)S(1)} %copy.110), channel_id=1, replica_groups=mesh['fsdp'=8,'replica'=4] {'replica'}, use_global_device_ids=true, to_apply=%region_17.18 | all-reduce | flops 1152 | bytes 9216 | tf_op jit(solution)/shard_map/psum | solution.py:244
  644.9 53.7 %reduce-scatter.24.cloned.1.call-done = f32[96,2304]{1,0:T(8,128)} async-done(((f32[768,2304]{1,0:T(8,128)}), f32[96,2304]{1,0:T(8,128)}) %reduce-scatter.24.cloned.1.call-update) | async-done | bytes 884752 | tf_op jit(solution)/shard_map/reduce_scatter | solution.py:224
  698.6 2.6 copy.101
  701.2 29.1 %all-gather.23.cloned.1.call-done = f32[384,768]{0,1:T(8,128)} async-done(((f32[384,192]{0,1:T(8,128)}), f32[384,768]{0,1:T(8,128)}) %all-gather.23.cloned.1.call-update) | async-done | bytes 1179664 | tf_op jit(solution)/shard_map/all_gather | solution.py:242
  730.3 4.7 fusion.12
  735.0 2.7 copy.99
  737.7 2.4 pad_maximum_fusion.1
  740.0 2.9 copy.100
  743.0 18.3 %all-gather.21.cloned.1.call-done = f32[96,3072]{1,0:T(8,128)} async-done(((f32[96,768]{1,0:T(8,128)}), f32[96,3072]{1,0:T(8,128)}) %all-gather.21.cloned.1.call-update) | async-done | bytes 1179664 | tf_op jit(solution)/shard_map/all_gather | solution.py:241
  761.2 3.4 fusion.15
  765.7 2.0 pad_maximum_fusion
  767.7 24.9 %reduce-scatter.34.cloned.1.call-done = f32[576,96]{1,0:T(8,128)} async-done(((f32[2304,96]{1,0:T(8,128)}), f32[576,96]{1,0:T(8,128)}) %reduce-scatter.34.cloned.1.call-update) | async-done | bytes 221200
  793.7 20.2 %all-gather.4 = f32[4,576,96]{1,2,0:T(8,128)S(1)} all-gather(f32[1,576,96]{1,2,0:T(8,128)S(1)} %bitcast.366), channel_id=1, replica_groups=mesh['fsdp'=8,'replica'=4] {'replica'}, dimensions={0}, use_global_device_ids=true | all-gather | bytes 1105920 | tf_op jit(solution)/shard_map/all_gather | solution.py:239
  820.7 2.6 fusion.21
  (245 shorter events, 58.9 us)
Async XLA Ops:
  7.2 23.7 %copy-start.1 = (bf16[1,128,768]{2,1,0:T(8,128)(2,1)S(1)}, bf16[1,128,768]{2,1,0:T(8,128)(2,1)}, u32[]{:S(2)}) copy-start(bf16[1,128,768]{2,1,0:T(8,128)(2,1)} %param.10) | copy-start | bytes 589828
  7.2 39.9 %all-gather.13.cloned.1.call-start = ((), (), s32[]{:S(2)}) async-start(), calls=%async_computation.11 | async-start | bytes 3981312 | tf_op jit(solution)/shard_map/all_gather | solution.py:122
  9.3 78.5 %all-gather.25.cloned.1.call-start = ((), (), s32[]{:S(2)}) async-start(), calls=%async_computation.23 | async-start | bytes 1966080 | tf_op jit(solution)/shard_map/all_gather | solution.py:145
  31.0 18.8 %copy-start.37 = (f32[128]{0:T(128)}, f32[128]{0:T(128)S(1)}, u32[]{:S(2)}) copy-start(f32[128]{0:T(128)S(1)} %broadcast_multiply_fusion.14) | copy-start | bytes 1540
  31.2 18.6 %copy-start.45 = (f32[128]{0:T(128)}, f32[128]{0:T(128)S(1)}, u32[]{:S(2)}) copy-start(f32[128]{0:T(128)S(1)} %add_rsqrt_fusion.1) | copy-start | bytes 1540
  50.6 62.5 %all-gather.15.cloned.1.call-start = ((), (), s32[]{:S(2)}) async-start(), calls=%async_computation.12 | async-start | bytes 1327104 | tf_op jit(solution)/shard_map/all_gather | solution.py:124
  52.3 101.9 %all-gather.17.cloned.1.call-start = ((), (), s32[]{:S(2)}) async-start(), calls=%async_computation.13 | async-start | bytes 5308416 | tf_op jit(solution)/shard_map/all_gather | solution.py:125
  54.5 141.6 %all-gather.19.cloned.1.call-start = ((), (), s32[]{:S(2)}) async-start(), calls=%async_computation.14 | async-start | bytes 5308416 | tf_op jit(solution)/shard_map/all_gather | solution.py:127
  58.6 13.3 %copy-start.3 = (f32[1,384,768]{1,2,0:T(8,128)}, f32[1,384,768]{1,2,0:T(8,128)S(1)}, u32[]{:S(2)}) copy-start(f32[1,384,768]{1,2,0:T(8,128)S(1)} %copy.111) | copy-start | bytes 3538948
  58.6 11.7 %copy-start.54 = (s32[1,512]{1,0:T(1,128)S(1)}, s32[1,512]{1,0:T(1,128)}, u32[]{:S(2)}) copy-start(s32[1,512]{1,0:T(1,128)} %param.12) | copy-start | bytes 6148
  59.6 216.8 %reduce-scatter.32.cloned.1.call-start = ((), (), s32[]{:S(2)}) async-start(), calls=%async_computation.21 | async-start | bytes 10616832 | tf_op jit(solution)/shard_map/reduce_scatter | solution.py:229
  163.8 158.8 %reduce-scatter.26.cloned.1.call-start = ((), (), s32[]{:S(2)}) async-start(), calls=%async_computation.17 | async-start | bytes 2654208 | tf_op jit(solution)/shard_map/reduce_scatter | solution.py:226
  196.1 5.3 copy-start.34
  196.1 5.3 copy-start.44
  201.4 5.1 copy-start.18
  201.4 5.1 copy-start.28
  201.4 6.6 copy-start.22
  210.0 193.0 %reduce-scatter.28.cloned.1.call-start = ((), (), s32[]{:S(2)}) async-start(), calls=%async_computation.18 | async-start | bytes 10616832 | tf_op jit(solution)/shard_map/reduce_scatter | solution.py:227
  217.3 249.0 %reduce-scatter.22.cloned.1.call-start = ((), (), s32[]{:S(2)}) async-start(), calls=%async_computation.15 | async-start | bytes 3932160 | tf_op jit(solution)/shard_map/reduce_scatter | solution.py:209
  229.6 268.2 %reduce-scatter.40.cloned.1.call-start = ((), (), s32[]{:S(2)}) async-start(), calls=%async_computation.27 | async-start | bytes 1474560
  279.0 124.0 %copy-start.42 = (f32[768]{0:T(1024)S(1)}, f32[768]{0:T(1024)}, u32[]{:S(2)}) copy-start(f32[768]{0:T(1024)} %get-tuple-element.163) | copy-start | bytes 9220
  279.0 124.1 %copy-start.40 = (f32[768]{0:T(1024)S(1)}, f32[768]{0:T(1024)}, u32[]{:S(2)}) copy-start(f32[768]{0:T(1024)} %get-tuple-element.129) | copy-start | bytes 9220
  279.0 124.1 %copy-start.39 = (f32[768]{0:T(1024)S(1)}, f32[768]{0:T(1024)}, u32[]{:S(2)}) copy-start(f32[768]{0:T(1024)} %get-tuple-element.135) | copy-start | bytes 9220
  279.0 124.1 %copy-start.41 = (f32[768]{0:T(1024)S(1)}, f32[768]{0:T(1024)}, u32[]{:S(2)}) copy-start(f32[768]{0:T(1024)} %get-tuple-element.184) | copy-start | bytes 9220
  279.0 124.1 %copy-start.7 = (bf16[512,768]{0,1:T(8,128)(2,1)S(1)}, bf16[512,768]{0,1:T(8,128)(2,1)}, u32[]{:S(2)}) copy-start(bf16[512,768]{0,1:T(8,128)(2,1)} %copy.86) | copy-start | bytes 2359300
  279.0 124.1 %copy-start.10 = (bf16[12,128,512]{2,1,0:T(8,128)(2,1)S(1)}, bf16[12,128,512]{2,1,0:T(8,128)(2,1)}, u32[]{:S(2)}) copy-start(bf16[12,128,512]{2,1,0:T(8,128)(2,1)} %copy-done.9) | copy-start | bytes 4718596
  279.1 252.4 %reduce-scatter.38.cloned.1.call-start = ((), (), s32[]{:S(2)}) async-start(), calls=%async_computation.26 | async-start | bytes 491520
  324.5 231.5 %reduce-scatter.30.cloned.1.call-start = ((), (), s32[]{:S(2)}) async-start(), calls=%async_computation.19 | async-start | bytes 1474560 | tf_op jit(solution)/shard_map/reduce_scatter | solution.py:235
  403.0 189.2 %reduce-scatter.36.cloned.1.call-start = ((), (), s32[]{:S(2)}) async-start(), calls=%async_computation.25 | async-start | bytes 442368
  468.9 160.8 %reduce-scatter.42.cloned.1.call-start = ((), (), s32[]{:S(2)}) async-start(), calls=%async_computation.28 | async-start | bytes 442368
  474.1 224.5 %reduce-scatter.24.cloned.1.call-start = ((), (), s32[]{:S(2)}) async-start(), calls=%async_computation.16 | async-start | bytes 7962624 | tf_op jit(solution)/shard_map/reduce_scatter | solution.py:224
  478.3 19.5 %copy-start.15 = (f32[1,384,768]{2,1,0:T(8,128)S(1)}, f32[1,384,768]{2,1,0:T(8,128)}, u32[]{:S(2)}) copy-start(f32[1,384,768]{2,1,0:T(8,128)} %get-tuple-element.169) | copy-start | bytes 3538948
  478.4 251.9 %all-gather.23.cloned.1.call-start = ((), (), s32[]{:S(2)}) async-start(), calls=%async_computation.22 | async-start | bytes 1474560 | tf_op jit(solution)/shard_map/all_gather | solution.py:242
  497.8 263.5 %all-gather.21.cloned.1.call-start = ((), (), s32[]{:S(2)}) async-start(), calls=%async_computation.20 | async-start | bytes 1474560 | tf_op jit(solution)/shard_map/all_gather | solution.py:241
  498.2 28.4 %copy-start.6 = (f32[128,3072]{1,0:T(8,128)S(1)}, f32[128,3072]{1,0:T(8,128)}, u32[]{:S(2)}) copy-start(f32[128,3072]{1,0:T(8,128)} %copy-done.5) | copy-start | bytes 4718596
  498.2 28.4 %copy-start.52 = (f32[768]{0:T(1024)S(1)}, f32[768]{0:T(1024)}, u32[]{:S(2)}) copy-start(f32[768]{0:T(1024)} %get-tuple-element.138) | copy-start | bytes 9220
  531.4 18.6 %copy-start.19 = (f32[3,96,768]{2,1,0:T(8,128)S(1)}, f32[3,96,768]{2,1,0:T(8,128)}, u32[]{:S(2)}) copy-start(f32[3,96,768]{2,1,0:T(8,128)} %param.15) | copy-start | bytes 2654212
  550.3 5.8 copy-start.12
  550.3 5.8 copy-start.23
  550.4 91.9 %copy-start.36 = (f32[384]{0:T(512)S(1)}, f32[384]{0:T(512)}, u32[]{:S(2)}) copy-start(f32[384]{0:T(512)} %copy-done.35) | copy-start | bytes 4612
  550.4 91.9 %copy-start.49 = (f32[384]{0:T(512)S(1)}, f32[384]{0:T(512)}, u32[]{:S(2)}) copy-start(f32[384]{0:T(512)} %get-tuple-element.143) | copy-start | bytes 4612
  550.5 91.9 %copy-start.50 = (f32[384]{0:T(512)S(1)}, f32[384]{0:T(512)}, u32[]{:S(2)}) copy-start(f32[384]{0:T(512)} %get-tuple-element.145) | copy-start | bytes 4612
  550.5 92.5 %copy-start.48 = (f32[3,2,96]{2,1,0:T(2,128)S(1)}, f32[3,2,96]{2,1,0:T(2,128)}, u32[]{:S(2)}) copy-start(f32[3,2,96]{2,1,0:T(2,128)} %param.14) | copy-start | bytes 6916
  550.5 93.8 %copy-start.30 = (f32[3,6,96]{2,1,0:T(8,128)S(1)}, f32[3,6,96]{2,1,0:T(8,128)}, u32[]{:S(2)}) copy-start(f32[3,6,96]{2,1,0:T(8,128)} %param.19) | copy-start | bytes 20740
  556.1 236.5 %reduce-scatter.34.cloned.1.call-start = ((), (), s32[]{:S(2)}) async-start(), calls=%async_computation.24 | async-start | bytes 1474560
  643.0 58.1 %copy-start.51 = (f32[2,96]{1,0:T(2,128)}, f32[2,96]{1,0:T(2,128)S(1)}, u32[]{:S(2)}) copy-start(f32[2,96]{1,0:T(2,128)S(1)} %get-tuple-element.162) | copy-start | bytes 2308
  644.2 56.9 %copy-start.43 = (f32[6,96]{1,0:T(8,128)}, f32[6,96]{1,0:T(8,128)S(1)}, u32[]{:S(2)}) copy-start(f32[6,96]{1,0:T(8,128)S(1)} %get-tuple-element.152) | copy-start | bytes 6916
  644.9 85.4 %copy-start.4 = (f32[1,384,768]{1,2,0:T(8,128)S(1)}, f32[1,384,768]{1,2,0:T(8,128)}, u32[]{:S(2)}) copy-start(f32[1,384,768]{1,2,0:T(8,128)} %copy-done.3) | copy-start | bytes 3538948
  (26 other events, 50.4 us)
Sparse Core Ops, SparseCore 0:
  10.5 36.5 all-gather.12
  50.7 37.0 all-gather.24
  90.2 22.7 all-gather.14
  115.4 38.7 all-gather.16
  156.5 39.6 all-gather.18
  199.5 76.8 reduce-scatter.31
  280.3 42.3 reduce-scatter.25
  326.1 76.8 reduce-scatter.27
  405.9 60.3 reduce-scatter.21
  468.5 29.2 reduce-scatter.39
  500.6 19.3 reduce-scatter.37
  522.2 33.8 reduce-scatter.29
  559.7 32.5 reduce-scatter.35
  595.7 33.8 reduce-scatter.41
  633.0 65.4 reduce-scatter.23
  700.0 30.2 all-gather.22
  731.7 29.4 all-gather.20
  764.0 28.5 reduce-scatter.33
where the time goes:
time: 833 us; the launch traced here: 832 us
  waiting for transfers between devices  571 us (69%)
  blocking collectives  103 us (12%)
  matrix products  56.1 us (7%)
  local copies, waits for them, and re-layouts  52.3 us (6%)
  other arithmetic  32.4 us (4%)
  between operations  15.8 us (2%)
    unnamed x23, waiting for transfers between devices  116 us
    reduce_scatter x1, waiting for transfers between devices, body(): lax.psum_scatter(grad_w_fc, 'fsdp', scatter_dimension=0, tiled=True)  78.4 us
    reduce_scatter x1, waiting for transfers between devices, body(): lax.psum_scatter(grad_kv_part, 'replica', scatter_dimension=1, tiled=True)  62.5 us
    reduce_scatter x1, waiting for transfers between devices, body(): lax.psum_scatter(grad_w_qkv, 'fsdp', scatter_dimension=0, tiled=True)  53.7 us
    reduce_scatter x1, waiting for transfers between devices, body(): lax.psum_scatter(grad_w_pr, 'fsdp', scatter_dimension=0, tiled=True)  46.7 us
    reduce_scatter x1, waiting for transfers between devices, body(): lax.psum_scatter(grad_w_out, 'fsdp', scatter_dimension=0, tiled=True)  43.5 us
    all_gather x1, waiting for transfers between devices, body(): lax.all_gather(w_fc_state[0].astype(jnp.bfloat16), 'fsdp', axis=0, tiled=...  38.1 us
    all_gather x1, waiting for transfers between devices, body(): lax.all_gather(w_pr_state[0].astype(jnp.bfloat16), 'fsdp', axis=0, tiled=...  32.1 us
  transfers between devices with their start and end apart: 18, of which 17 were waited for; matrix products, arithmetic and copies ran while one was open for 14% of the time, Pallas kernels for 0%

commit v1 on v0

--- a/solution.py
+++ b/solution.py
@@ -106,6 +106,18 @@
     return (grad_query.reshape(rows, -1), grad_kv)
 
 
+def map_sequences(function, elements):
+    if elements[0].shape[0] == 1:
+        return jax.tree.map(lambda x: x[None], function([x[0] for x in elements]))
+    return lax.map(function, elements)
+
+
+def reduce_matrix(grad):
+    part = lax.psum_scatter(grad.astype(jnp.bfloat16), "fsdp", scatter_dimension=0, tiled=True)
+    part = lax.psum_scatter(part, "replica", scatter_dimension=1, tiled=True)
+    return lax.all_gather(part, "replica", axis=1, tiled=True).astype(jnp.float32)
+
+
 def body(
     inputs,
     cotangent,
@@ -118,16 +130,19 @@
     w_pr_state,
     vec_state,
 ):
-    gathered = (
-        lax.all_gather(w_qkv_state[0].astype(jnp.bfloat16), "fsdp", axis=0, tiled=True),
-        lax.all_gather(b_qkv_state[0].astype(jnp.bfloat16), "fsdp", axis=1, tiled=True),
-        lax.all_gather(w_o_state[0].astype(jnp.bfloat16), "fsdp", axis=0, tiled=True),
-        lax.all_gather(w_fc_state[0].astype(jnp.bfloat16), "fsdp", axis=0, tiled=True),
-        lax.all_gather(b_fc_state[0].astype(jnp.bfloat16), "fsdp", axis=0, tiled=True),
-        lax.all_gather(w_pr_state[0].astype(jnp.bfloat16), "fsdp", axis=0, tiled=True),
-        lax.all_gather(vec_state[0].astype(jnp.bfloat16), "fsdp", axis=1, tiled=True),
-    )
-    w_qkv, b_qkv, w_out, w_fc, b_fc, w_pr, vectors = gathered
+    shard = vec_state.shape[2]
+    hidden_ratio = b_fc_state.shape[1] // shard
+    small = jnp.concatenate(
+        [vec_state[0], b_qkv_state[0], b_fc_state[0].reshape(hidden_ratio, shard)], 0
+    ).astype(jnp.bfloat16)
+    small_all = lax.all_gather(small, "fsdp", axis=0, tiled=False)
+    w_qkv = lax.all_gather(w_qkv_state[0].astype(jnp.bfloat16), "fsdp", axis=0, tiled=True)
+    w_out = lax.all_gather(w_o_state[0].astype(jnp.bfloat16), "fsdp", axis=0, tiled=True)
+    w_fc = lax.all_gather(w_fc_state[0].astype(jnp.bfloat16), "fsdp", axis=0, tiled=True)
+    w_pr = lax.all_gather(w_pr_state[0].astype(jnp.bfloat16), "fsdp", axis=0, tiled=True)
+    vectors = small_all[:, :6].transpose(1, 0, 2).reshape(6, -1)
+    b_qkv = small_all[:, 6:8].transpose(1, 0, 2).reshape(2, -1)
+    b_fc = small_all[:, 8:].reshape(-1)
     vector_f = vectors.astype(jnp.float32)
     bias_row = jnp.concatenate([b_qkv[0], jnp.zeros_like(b_qkv[0]), b_qkv[1]]).astype(jnp.float32)
     seq_count, span, width = inputs.shape
@@ -150,7 +165,7 @@
     def forward_one(element):
         return attend_forward(element[0], element[1], element[2], element[3], pos_query, pos_all)
 
-    attended, log_norm = lax.map(forward_one, (queries, key_value_all, seg_query, segments))
+    attended, log_norm = map_sequences(forward_one, (queries, key_value_all, seg_query, segments))
     attended_rows = attended.reshape(row_count, width)
     mixed = hidden + jnp.dot(attended_rows, w_out, preferred_element_type=jnp.float32) + vector_f[2]
     ffn_in_f, normed_two, scale_two = layer_norm(mixed, vector_f[3], vector_f[4])
@@ -159,17 +174,7 @@
     activ, slope = gelu_parts(pre_act)
     activ_b = activ.astype(jnp.bfloat16)
     result = mixed + jnp.dot(activ_b, w_pr, preferred_element_type=jnp.float32) + vector_f[5]
-    back_weights = (
-        lax.all_gather(w_qkv_state[0].astype(jnp.bfloat16), "fsdp", axis=0, tiled=True),
-        lax.all_gather(b_qkv_state[0].astype(jnp.bfloat16), "fsdp", axis=1, tiled=True),
-        lax.all_gather(w_o_state[0].astype(jnp.bfloat16), "fsdp", axis=0, tiled=True),
-        lax.all_gather(w_fc_state[0].astype(jnp.bfloat16), "fsdp", axis=0, tiled=True),
-        lax.all_gather(b_fc_state[0].astype(jnp.bfloat16), "fsdp", axis=0, tiled=True),
-        lax.all_gather(w_pr_state[0].astype(jnp.bfloat16), "fsdp", axis=0, tiled=True),
-        lax.all_gather(vec_state[0].astype(jnp.bfloat16), "fsdp", axis=1, tiled=True),
-    )
-    back_qkv, back_bias_qkv, back_out, back_fc, back_bias_fc, back_pr, back_vectors = back_weights
-    back_vec_f = back_vectors.astype(jnp.float32)
+    back_qkv, back_out, back_fc, back_pr, back_vec_f = (w_qkv, w_out, w_fc, w_pr, vector_f)
     cot_rows = cotangent.reshape(row_count, width)
     cot_f = cot_rows.astype(jnp.float32)
     grad_w_pr = jnp.dot(activ_b.T, cot_rows, preferred_element_type=jnp.float32)
@@ -203,10 +208,12 @@
             element[6],
         )
 
-    grad_query, grad_kv_part = lax.map(
+    grad_query, grad_kv_part = map_sequences(
         backward_one, (queries, key_value_all, seg_query, segments, log_norm, attended, grad_att)
     )
-    grad_kv = lax.psum_scatter(grad_kv_part, "replica", scatter_dimension=1, tiled=True)
+    grad_kv = lax.psum_scatter(
+        grad_kv_part.astype(jnp.bfloat16), "replica", scatter_dimension=1, tiled=True
+    ).astype(jnp.float32)
     grad_proj = jnp.concatenate([grad_query, grad_kv], 2).reshape(row_count, 3 * width)
     grad_proj_b = grad_proj.astype(jnp.bfloat16)
     grad_b_qkv = jnp.stack(
@@ -220,36 +227,25 @@
     grad_vec = jnp.stack(
         [grad_gain_one, grad_bias_one, grad_b_out, grad_gain_two, grad_bias_two, grad_b_pr]
     )
-    shares = (
-        lax.psum_scatter(grad_w_qkv, "fsdp", scatter_dimension=0, tiled=True),
-        lax.psum_scatter(grad_b_qkv, "fsdp", scatter_dimension=1, tiled=True),
-        lax.psum_scatter(grad_w_out, "fsdp", scatter_dimension=0, tiled=True),
-        lax.psum_scatter(grad_w_fc, "fsdp", scatter_dimension=0, tiled=True),
-        lax.psum_scatter(grad_b_fc, "fsdp", scatter_dimension=0, tiled=True),
-        lax.psum_scatter(grad_w_pr, "fsdp", scatter_dimension=0, tiled=True),
-        lax.psum_scatter(grad_vec, "fsdp", scatter_dimension=1, tiled=True),
-    )
-    matrix_parts = (
-        lax.psum_scatter(shares[0], "replica", scatter_dimension=1, tiled=True),
-        lax.psum_scatter(shares[2], "replica", scatter_dimension=1, tiled=True),
-        lax.psum_scatter(shares[3], "replica", scatter_dimension=1, tiled=True),
-        lax.psum_scatter(shares[5], "replica", scatter_dimension=1, tiled=True),
-    )
-    matrix_sums = (
-        lax.all_gather(matrix_parts[0], "replica", axis=1, tiled=True),
-        lax.all_gather(matrix_parts[1], "replica", axis=1, tiled=True),
-        lax.all_gather(matrix_parts[2], "replica", axis=1, tiled=True),
-        lax.all_gather(matrix_parts[3], "replica", axis=1, tiled=True),
-    )
-    small_sums = lax.psum((shares[1], shares[4], shares[6]), "replica")
+    groups = lax.axis_size("fsdp")
+    small_grads = jnp.concatenate(
+        [
+            grad_vec.reshape(6, groups, shard).transpose(1, 0, 2),
+            grad_b_qkv.reshape(2, groups, shard).transpose(1, 0, 2),
+            grad_b_fc.reshape(groups, hidden_ratio, shard),
+        ],
+        1,
+    )
+    small_sums = lax.psum(small_grads, ("fsdp", "replica"))
+    small_own = lax.dynamic_index_in_dim(small_sums, lax.axis_index("fsdp"), 0, keepdims=False)
     totals = (
-        matrix_sums[0],
-        small_sums[0],
-        matrix_sums[1],
-        matrix_sums[2],
-        small_sums[1],
-        matrix_sums[3],
-        small_sums[2],
+        reduce_matrix(grad_w_qkv),
+        small_own[6:8],
+        reduce_matrix(grad_w_out),
+        reduce_matrix(grad_w_fc),
+        small_own[8:].reshape(-1),
+        reduce_matrix(grad_w_pr),
+        small_own[:6],
     )
     factor = float(row_count * lax.axis_size("fsdp") * lax.axis_size("replica")) ** (-0.5)
     grads = [total * factor for total in totals]

time: 833 us -> 593 us (0.71)
  waiting for transfers between devices: 571 us -> 305 us
  local copies, waits for them, and re-layouts: 52.3 us -> 64.6 us
  blocking collectives: 103 us -> 113 us
    reduce_scatter x6 -> x5, waiting for transfers between devices: 289 us -> 111 us  [the longest x4 111 us: reduce_matrix(): lax.psum_scatter(grad.astype(jnp.bfloat16), 'fsdp', scatter_dimension=0,...]
    unnamed x23 -> x18, waiting for transfers between devices: 116 us -> 52.8 us
    all_gather x2 -> x0, waiting for transfers between devices: 47.4 us -> none  [the longest x1 29.1 us: body(): lax.all_gather(matrix_parts[3], 'replica', axis=1, tiled=True)]
    psum x1, blocking collectives: 11.8 us -> 39.8 us  [body(): small_sums = lax.psum(small_grads, ('fsdp', 'replica'))]
    unnamed x1 -> x0, blocking collectives: 24.3 us -> none
    all_gather x1, waiting for transfers between devices: 15.9 us -> 25 us  [body(): key_value_all = lax.all_gather(key_value, 'replica', axis=1, tiled=True)]
    another operation x17 -> x13, other arithmetic: 20.5 us -> 21.4 us  [adamw(): return jnp.stack([weight, first, second])]
    unnamed x131 -> x109, local copies, waits for them, and re-layouts: 28.2 us -> 28.7 us
  transfers between devices with their start and end apart: 18 -> 14, of which waited for: 17 -> 11; matrix products, arithmetic and copies ran while one was open for 14% -> 21% of each run, Pallas kernels for 0% -> 0%
where the time goes in v1:
time: 593 us; the launch traced here: 591 us
  waiting for transfers between devices  305 us (51%)
  blocking collectives  113 us (19%)
  local copies, waits for them, and re-layouts  64.6 us (11%)
  matrix products  56.1 us (9%)
  other arithmetic  37.2 us (6%)
  between operations  14.5 us (2%)
    reduce_scatter x4, waiting for transfers between devices, reduce_matrix(): lax.psum_scatter(grad.astype(jnp.bfloat16), 'fsdp', scatter_dimension=0,...  111 us
    all_gather x4, blocking collectives, reduce_matrix(): lax.all_gather(part, 'replica', axis=1, tiled=True).astype(jnp.float32)  62.6 us
    unnamed x18, waiting for transfers between devices  52.8 us
    psum x1, blocking collectives, body(): small_sums = lax.psum(small_grads, ('fsdp', 'replica'))  39.8 us
    all_gather x1, waiting for transfers between devices, body(): lax.all_gather(w_fc_state[0].astype(jnp.bfloat16), 'fsdp', axis=0, tiled=...  38.1 us
    all_gather x1, waiting for transfers between devices, body(): lax.all_gather(w_pr_state[0].astype(jnp.bfloat16), 'fsdp', axis=0, tiled=...  37.6 us
    unnamed x109, local copies, waits for them, and re-layouts  28.7 us
    all_gather x1, waiting for transfers between devices, body(): key_value_all = lax.all_gather(key_value, 'replica', axis=1, tiled=True)  25 us
  transfers between devices with their start and end apart: 14, of which 11 were waited for; matrix products, arithmetic and copies ran while one was open for 21% of the time, Pallas kernels for 0%

profile of v1, /device:TPU:0, one launch (start us, length us, event | category | flops | bytes accessed | tf_op | source)
XLA Modules:
  0.0 591.3 jit_solution(13273350319115519774)
XLA Ops:
  7.2 2.0 bitcast_convert_fusion.2
  11.5 10.6 %all_gather.31 = bf16[8,12,96]{2,1,0:T(8,128)(2,1)S(1)} all-gather(bf16[1,12,96]{2,1,0:T(8,128)(2,1)S(1)} %pad_maximum_fusion.8), channel_id=1, replica_groups=mesh['fsdp'=8,'replica'=4] {'fsdp'}, dimensions={0}, use_global_device_ids=true | all-gather | bytes 20736 | tf_op jit(solution)/shard_map/all_gather | solution.py:138
  23.5 23.6 %all-gather.8.cloned.1.call-done = bf16[768,2304]{1,0:T(8,128)(2,1)} async-done(((bf16[96,2304]{1,0:T(8,128)(2,1)}), bf16[768,2304]{1,0:T(8,128)(2,1)}) %all-gather.8.cloned.1.call-update) | async-done | bytes 3538960 | tf_op jit(solution)/shard_map/all_gather | solution.py:139
  47.0 2.7 fusion
  52.3 2.2 bitcast_convert_fusion.1
  54.6 3.7 fusion.96
  62.8 25.0 %all-gather.16.cloned.1.call-done = bf16[512,1536]{1,0:T(8,128)(2,1)} async-done(((bf16[128,1536]{1,0:T(8,128)(2,1)}), bf16[512,1536]{1,0:T(8,128)(2,1)}) %all-gather.16.cloned.1.call-update) | async-done | bytes 1572880 | tf_op jit(solution)/shard_map/all_gather | solution.py:160
  91.5 1.9 fusion.2
  96.6 16.4 %all-gather.10.cloned.1.call-done = bf16[768,768]{1,0:T(8,128)(2,1)} async-done(((bf16[96,768]{1,0:T(8,128)(2,1)}), bf16[768,768]{1,0:T(8,128)(2,1)}) %all-gather.10.cloned.1.call-update) | async-done | bytes 1179664 | tf_op jit(solution)/shard_map/all_gather | solution.py:140
  113.0 1.8 fusion.98
  116.1 38.1 %all-gather.12.cloned.1.call-done = bf16[768,3072]{1,0:T(8,128)(2,1)} async-done(((bf16[96,3072]{1,0:T(8,128)(2,1)}), bf16[768,3072]{1,0:T(8,128)(2,1)}) %all-gather.12.cloned.1.call-update) | async-done | bytes 4718608 | tf_op jit(solution)/shard_map/all_gather | solution.py:141
  154.2 4.4 convolution_add_fusion.1
  158.5 37.6 %all-gather.14.cloned.1.call-done = bf16[3072,768]{0,1:T(8,128)(2,1)} async-done(((bf16[384,768]{0,1:T(8,128)(2,1)}), bf16[3072,768]{0,1:T(8,128)(2,1)}) %all-gather.14.cloned.1.call-update) | async-done | bytes 4718608 | tf_op jit(solution)/shard_map/all_gather | solution.py:142
  196.1 5.4 fusion.99
  201.6 2.3 multiply_reduce_fusion
  207.2 5.3 convolution_convert_fusion
  212.6 4.8 convolution_convert_fusion.1
  217.5 2.7 convolution_convert_fusion.6
  220.1 1.7 copy.63
  223.0 2.9 convolution_convert_fusion.4
  225.9 2.2 multiply_convert_fusion
  228.1 15.6 %reduce-scatter.20.cloned.1.call-done = bf16[96,768]{1,0:T(8,128)(2,1)} async-done(((bf16[768,768]{1,0:T(8,128)(2,1)}), bf16[96,768]{1,0:T(8,128)(2,1)}) %reduce-scatter.20.cloned.1.call-update) | async-done | bytes 147472 | tf_op jit(solution)/shard_map/reduce_scatter | solution.py:116
  245.6 1.9 convolution_convert_fusion.5
  248.7 7.1 %copy.74 = bf16[1,512,1536]{2,0,1:T(2,128)(2,1)S(1)} copy(bf16[1,512,1536]{1,2,0:T(8,128)(2,1)} %pad_maximum_fusion.3) | data formatting | bytes 3145728
  257.4 43.7 %reduce-scatter.26.cloned.1.call-done = bf16[384,768]{1,0:T(8,128)(2,1)} async-done(((bf16[3072,768]{1,0:T(8,128)(2,1)}), bf16[384,768]{1,0:T(8,128)(2,1)}) %reduce-scatter.26.cloned.1.call-update) | async-done | bytes 589840 | tf_op jit(solution)/shard_map/reduce_scatter | solution.py:116
  301.0 2.1 copy.80
  306.1 52.2 %reduce-scatter.22.cloned.1.call-done = bf16[96,3072]{1,0:T(8,128)(2,1)} async-done(((bf16[768,3072]{1,0:T(8,128)(2,1)}), bf16[96,3072]{1,0:T(8,128)(2,1)}) %reduce-scatter.22.cloned.1.call-update) | async-done | bytes 589840 | tf_op jit(solution)/shard_map/reduce_scatter | solution.py:116
  358.4 2.9 bitcast_convert_fusion.3
  364.7 4.8 fusion.23
  369.5 11.2 %reduce-scatter.32.cloned.1.call-done = bf16[192,96]{1,0:T(8,128)(2,1)} async-done(((bf16[768,96]{1,0:T(8,128)(2,1)}), bf16[192,96]{1,0:T(8,128)(2,1)}) %reduce-scatter.32.cloned.1.call-update) | async-done | bytes 36880
  380.7 14.9 %all_gather.38 = bf16[96,768]{0,1:T(8,128)(2,1)S(1)} all-gather(bf16[96,192]{0,1:T(8,128)(2,1)} %bitcast.305), channel_id=1, replica_groups=mesh['fsdp'=8,'replica'=4] {'replica'}, dimensions={1}, use_global_device_ids=true | all-gather | bytes 184320 | tf_op jit(solution)/shard_map/all_gather | solution.py:118
  395.8 22.0 %reduce-scatter.28.cloned.1.call-done = bf16[128,1536]{1,0:T(8,128)(2,1)} async-done(((bf16[512,1536]{1,0:T(8,128)(2,1)}), bf16[128,1536]{1,0:T(8,128)(2,1)}) %reduce-scatter.28.cloned.1.call-update) | async-done | bytes 393232
  419.8 3.0 convolution_convert_fusion.2
  427.9 3.9 fusion.50
  435.7 39.8 %psum.7 = f32[8,12,96]{2,1,0:T(8,128)S(1)} all-reduce(f32[8,12,96]{2,1,0:T(8,128)S(1)} %pad_maximum_fusion.5), channel_id=1, replica_groups=mesh['fsdp'=8,'replica'=4] {'fsdp','replica'}, use_global_device_ids=true, to_apply=%region_23.24 | all-reduce | flops 9216 | bytes 73728 | tf_op jit(solution)/shard_map/psum | solution.py:239
  483.0 2.1 fusion.70
  485.1 16.1 %all_gather.40 = bf16[384,768]{0,1:T(8,128)(2,1)S(1)} all-gather(bf16[384,192]{0,1:T(8,128)(2,1)} %bitcast.303), channel_id=1, replica_groups=mesh['fsdp'=8,'replica'=4] {'replica'}, dimensions={1}, use_global_device_ids=true | all-gather | bytes 737280 | tf_op jit(solution)/shard_map/all_gather | solution.py:118
  501.2 3.7 fusion.18
  506.4 2.5 pad_maximum_fusion.1
  508.8 2.9 copy.73
  511.8 15.5 %all_gather.39 = bf16[96,3072]{1,0:T(8,128)(2,1)S(1)} all-gather(bf16[96,768]{1,0:T(8,128)(2,1)} %reduce-scatter.24.cloned.1.call-done), channel_id=1, replica_groups=mesh['fsdp'=8,'replica'=4] {'replica'}, dimensions={1}, use_global_device_ids=true | all-gather | bytes 737280 | tf_op jit(solution)/shard_map/all_gather | solution.py:118
  527.3 3.9 fusion.21
  531.2 2.1 copy.76
  533.3 1.8 fusion.67
  535.2 2.0 pad_maximum_fusion
  537.2 19.4 %reduce-scatter.30.cloned.1.call-done = bf16[576,96]{1,0:T(8,128)(2,1)} async-done(((bf16[2304,96]{1,0:T(8,128)(2,1)}), bf16[576,96]{1,0:T(8,128)(2,1)}) %reduce-scatter.30.cloned.1.call-update) | async-done | bytes 110608
  557.6 16.0 %all-gather.1 = bf16[4,576,96]{1,2,0:T(8,128)(2,1)S(1)} all-gather(bf16[1,576,96]{1,2,0:T(8,128)(2,1)S(1)} %bitcast.301), channel_id=1, replica_groups=mesh['fsdp'=8,'replica'=4] {'replica'}, dimensions={0}, use_global_device_ids=true | all-gather | bytes 552960 | tf_op jit(solution)/shard_map/all_gather | solution.py:118
  580.4 2.6 fusion.27
  (222 shorter events, 63.6 us)
Async XLA Ops:
  7.2 16.0 %copy-start.5 = (bf16[1,128,768]{2,1,0:T(8,128)(2,1)S(1)}, bf16[1,128,768]{2,1,0:T(8,128)(2,1)}, u32[]{:S(2)}) copy-start(bf16[1,128,768]{2,1,0:T(8,128)(2,1)} %param.10) | copy-start | bytes 589828
  7.2 39.9 %all-gather.8.cloned.1.call-start = ((), (), s32[]{:S(2)}) async-start(), calls=%async_computation.9 | async-start | bytes 3981312 | tf_op jit(solution)/shard_map/all_gather | solution.py:139
  9.3 78.5 %all-gather.16.cloned.1.call-start = ((), (), s32[]{:S(2)}) async-start(), calls=%async_computation.18 | async-start | bytes 1966080 | tf_op jit(solution)/shard_map/all_gather | solution.py:160
  23.3 26.5 %copy-start.39 = (f32[128]{0:T(128)}, f32[128]{0:T(128)S(1)}, u32[]{:S(2)}) copy-start(f32[128]{0:T(128)S(1)} %broadcast_multiply_fusion.7) | copy-start | bytes 1540
  23.5 26.3 %copy-start.43 = (f32[128]{0:T(128)}, f32[128]{0:T(128)S(1)}, u32[]{:S(2)}) copy-start(f32[128]{0:T(128)S(1)} %add_rsqrt_fusion.1) | copy-start | bytes 1540
  50.6 62.5 %all-gather.10.cloned.1.call-start = ((), (), s32[]{:S(2)}) async-start(), calls=%async_computation.10 | async-start | bytes 1327104 | tf_op jit(solution)/shard_map/all_gather | solution.py:140
  52.3 101.9 %all-gather.12.cloned.1.call-start = ((), (), s32[]{:S(2)}) async-start(), calls=%async_computation.11 | async-start | bytes 5308416 | tf_op jit(solution)/shard_map/all_gather | solution.py:141
  54.5 141.6 %all-gather.14.cloned.1.call-start = ((), (), s32[]{:S(2)}) async-start(), calls=%async_computation.12 | async-start | bytes 5308416 | tf_op jit(solution)/shard_map/all_gather | solution.py:142
  58.6 4.2 copy-start.3
  58.6 2.6 copy-start.47
  59.6 184.2 %reduce-scatter.20.cloned.1.call-start = ((), (), s32[]{:S(2)}) async-start(), calls=%async_computation.14 | async-start | bytes 1327104 | tf_op jit(solution)/shard_map/reduce_scatter | solution.py:116
  196.1 5.4 copy-start
  196.1 5.4 copy-start.30
  196.1 5.4 copy-start.41
  201.5 2.4 copy-start.18
  201.6 2.4 copy-start.26
  201.6 3.9 copy-start.20
  207.0 94.1 %reduce-scatter.26.cloned.1.call-start = ((), (), s32[]{:S(2)}) async-start(), calls=%async_computation.17 | async-start | bytes 5308416 | tf_op jit(solution)/shard_map/reduce_scatter | solution.py:116
  212.5 145.8 %reduce-scatter.22.cloned.1.call-start = ((), (), s32[]{:S(2)}) async-start(), calls=%async_computation.15 | async-start | bytes 5308416 | tf_op jit(solution)/shard_map/reduce_scatter | solution.py:116
  217.4 5.5 copy-start.46
  217.4 163.3 %reduce-scatter.32.cloned.1.call-start = ((), (), s32[]{:S(2)}) async-start(), calls=%async_computation.21 | async-start | bytes 245760
  223.0 2.9 copy-start.23
  223.0 2.9 copy-start.24
  223.0 2.9 copy-start.28
  228.1 19.3 %copy-start.25 = (bf16[12,64,512]{2,1,0:T(8,128)(2,1)S(1)}, bf16[12,64,512]{2,1,0:T(8,128)(2,1)}, u32[]{:S(2)}) copy-start(bf16[12,64,512]{2,1,0:T(8,128)(2,1)} %convolution_convert_fusion.4) | copy-start | bytes 2359300
  245.5 172.2 %reduce-scatter.28.cloned.1.call-start = ((), (), s32[]{:S(2)}) async-start(), calls=%async_computation.19 | async-start | bytes 1966080
  257.3 45.9 %copy-start.38 = (f32[8,96]{1,0:T(8,128)S(1)}, f32[8,96]{1,0:T(8,128)}, u32[]{:S(2)}) copy-start(f32[8,96]{1,0:T(8,128)} %get-tuple-element.59) | copy-start | bytes 9220
  257.3 46.0 %copy-start.12 = (f32[1,384,768]{2,1,0:T(8,128)S(1)}, f32[1,384,768]{2,1,0:T(8,128)}, u32[]{:S(2)}) copy-start(f32[1,384,768]{2,1,0:T(8,128)} %get-tuple-element.84) | copy-start | bytes 3538948
  257.3 227.8 %reduce-scatter.34.cloned.1.call-start = ((), (), s32[]{:S(2)}) async-start(), calls=%async_computation.22 | async-start | bytes 737280
  303.2 208.6 %reduce-scatter.24.cloned.1.call-start = ((), (), s32[]{:S(2)}) async-start(), calls=%async_computation.16 | async-start | bytes 737280 | tf_op jit(solution)/shard_map/reduce_scatter | solution.py:117
  304.7 53.7 %copy-start.7 = (bf16[512,768]{0,1:T(8,128)(2,1)S(1)}, bf16[512,768]{0,1:T(8,128)(2,1)}, u32[]{:S(2)}) copy-start(bf16[512,768]{0,1:T(8,128)(2,1)} %copy.61) | copy-start | bytes 2359300
  358.3 3.0 copy-start.42
  358.3 3.7 copy-start.34
  358.3 4.4 copy-start.32
  358.3 5.0 copy-start.31
  358.4 5.7 copy-start.33
  358.4 6.3 %copy-start.2 = (f32[128,3072]{1,0:T(8,128)S(1)}, f32[128,3072]{1,0:T(8,128)}, u32[]{:S(2)}) copy-start(f32[128,3072]{1,0:T(8,128)} %convolution_add_fusion.1) | copy-start | bytes 4718596
  358.4 172.8 %reduce-scatter.18.cloned.1.call-start = ((), (), s32[]{:S(2)}) async-start(), calls=%async_computation.13 | async-start | bytes 3981312 | tf_op jit(solution)/shard_map/reduce_scatter | solution.py:116
  369.5 50.3 %copy-start.6 = (bf16[1,128,768]{2,1,0:T(8,128)(2,1)S(1)}, bf16[1,128,768]{2,1,0:T(8,128)(2,1)}, u32[]{:S(2)}) copy-start(bf16[1,128,768]{2,1,0:T(8,128)(2,1)} %param.10) | copy-start | bytes 589828
  369.5 50.3 %copy-start.40 = (f32[128]{0:T(128)S(1)}, f32[128]{0:T(128)}, u32[]{:S(2)}) copy-start(f32[128]{0:T(128)} %copy-done.39) | copy-start | bytes 1540
  369.5 50.3 %copy-start.44 = (f32[128]{0:T(128)S(1)}, f32[128]{0:T(128)}, u32[]{:S(2)}) copy-start(f32[128]{0:T(128)} %copy-done.43) | copy-start | bytes 1540
  419.8 3.1 copy-start.14
  422.9 133.7 %reduce-scatter.30.cloned.1.call-start = ((), (), s32[]{:S(2)}) async-start(), calls=%async_computation.20 | async-start | bytes 737280
  427.9 5.6 copy-start.35
  427.9 5.6 copy-start.36
  427.9 5.6 copy-start.37
  431.8 69.4 %copy-start.4 = (f32[1,384,768]{1,2,0:T(8,128)S(1)}, f32[1,384,768]{1,2,0:T(8,128)}, u32[]{:S(2)}) copy-start(f32[1,384,768]{1,2,0:T(8,128)} %copy-done.3) | copy-start | bytes 3538948
  431.8 69.4 %copy-start.10 = (f32[1,384,768]{1,2,0:T(8,128)S(1)}, f32[1,384,768]{1,2,0:T(8,128)}, u32[]{:S(2)}) copy-start(f32[1,384,768]{1,2,0:T(8,128)} %copy.84) | copy-start | bytes 3538948
  (14 other events, 19.1 us)
Sparse Core Ops, SparseCore 0:
  10.5 36.5 all-gather.7
  50.7 37.0 all-gather.15
  90.2 22.7 all-gather.9
  115.3 38.7 all-gather.11
  156.4 39.6 all-gather.13
  207.1 36.6 reduce-scatter.19
  247.2 53.7 reduce-scatter.25
  304.5 53.7 reduce-scatter.21
  361.1 19.5 reduce-scatter.31
  383.4 34.2 reduce-scatter.27
  420.0 21.4 reduce-scatter.33
  443.7 21.1 reduce-scatter.23
  468.9 46.1 reduce-scatter.17
  533.4 23.1 reduce-scatter.29
